TPU v7x, 512 devices: a whole 4x8x8 slice. The times are simulated.
512 devices in a mesh: row: 32 (over y, x_hi, core), col: 16 (over x_lo, z).
Axes of the slice: x: 4 (x_hi: 2, x_lo: 2; x = x_hi * 2 + x_lo), y: 8, z: 8, core: 2. Of those that a mesh axis runs over, the one named last changes fastest.
Arguments:
- tile_blocks: bfloat16 [12288, 128, 128], P(('row', 'col')), may hold values from -0.21875 to 0.21875
- tile_rows: int32 [12288], P(('row', 'col')), may hold values from 0 to 4095, as said below
- tile_cols: int32 [12288], P(('row', 'col')), may hold values from 0 to 4095, as said below
- trial_vectors: bfloat16 [4, 524288], P(None, ('col', 'row')), may hold values from -6 to 6
- basis_old: float32 [44, 524288], P(None, ('col', 'row'))
- image_old: float32 [44, 524288], P(None, ('col', 'row'))
Outputs:
- projected: float32 [48, 48], replicated
- basis_new: float32 [48, 524288], P(None, ('col', 'row'))
- image_new: float32 [48, 524288], P(None, ('col', 'row'))
Inputs may be any that keep to these rules, and one draw needn't show every extreme that they name: `tile_rows`: the 24 tiles of each device with index r on row have block rows b for which (b // 8) % 32 equals r. `tile_cols`: the 24 tiles of each device with index c on col have block columns from c * 256 to (c + 1) * 256 - 1.
All inputs are finite; a program needn't handle non-finite values.
Results may differ from a plain program's by a relative error of at most 0.0003.
Values may be sent and summed in bfloat16 or wider, within the bound.
A program may use at most 64 MiB of HBM per device.

v0:
```python
import jax
import jax.numpy as jnp
from jax import lax
from jax.sharding import PartitionSpec as P


def rows_product(left, right):
    return lax.dot_general(left, right, (((1,), (1,)), ((), ())), precision=lax.Precision.HIGHEST)


def place_blocks(local_index, block_count, products):
    onehot = (local_index[None, :] == jnp.arange(block_count, dtype=jnp.int32)[:, None]).astype(
        jnp.float32
    )
    flat = products.reshape(products.shape[0], -1)
    placed = jnp.dot(onehot, flat, precision=lax.Precision.HIGHEST)
    return placed.reshape(block_count, products.shape[1], products.shape[2])


def local(tile_blocks, tile_rows, tile_cols, trial_vectors, basis_old, image_old):
    tile_size = tile_blocks.shape[1]
    piece_width = trial_vectors.shape[1]
    vec_count = trial_vectors.shape[0]
    blocks_dev = piece_width // tile_size
    n_row = lax.axis_size("row")
    n_col = lax.axis_size("col")
    row_blocks = blocks_dev * n_col
    col_blocks = blocks_dev * n_row
    row_index = lax.axis_index("row")
    col_index = lax.axis_index("col")
    all_rows = float(piece_width * n_row * n_col)
    gathered = lax.all_gather(trial_vectors, ("row", "col"), axis=1, tiled=True)
    grid = gathered.reshape(vec_count, n_row, n_col, piece_width)
    col_vectors = lax.dynamic_index_in_dim(grid, col_index, 2, keepdims=False).reshape(
        vec_count, -1
    )
    row_vectors = lax.dynamic_index_in_dim(grid, row_index, 1, keepdims=False).reshape(
        vec_count, -1
    )
    local_rows = tile_rows // blocks_dev // n_row * blocks_dev + tile_rows % blocks_dev
    local_cols = tile_cols - col_index * col_blocks
    picked_cols = jnp.take(
        col_vectors.reshape(vec_count, col_blocks, tile_size), local_cols, axis=1
    )
    forward = jnp.einsum(
        "ktb,tab->tka", picked_cols, tile_blocks, preferred_element_type=jnp.float32
    )
    picked_rows = jnp.take(
        row_vectors.reshape(vec_count, row_blocks, tile_size), local_rows, axis=1
    )
    backward = jnp.einsum(
        "kta,tab->tkb", picked_rows, tile_blocks, preferred_element_type=jnp.float32
    )
    row_partial = place_blocks(local_rows, row_blocks, forward)
    col_partial = place_blocks(local_cols, col_blocks, backward)
    col_share = lax.psum_scatter(col_partial, "row", scatter_dimension=0, tiled=True)
    row_total = lax.psum(row_partial, "col")
    own_rows = lax.dynamic_slice_in_dim(row_total, col_index * blocks_dev, blocks_dev, 0)
    new_image = (own_rows + col_share).transpose(1, 0, 2).reshape(vec_count, piece_width)
    trial_wide = trial_vectors.astype(jnp.float32)
    basis_all = jnp.concatenate([basis_old, trial_wide], axis=0)
    images_all = jnp.concatenate([image_old, new_image], axis=0)
    correlation, coupling = lax.psum(
        (rows_product(basis_all, basis_all), rows_product(basis_all, images_all)), ("row", "col")
    )
    correlation = correlation / all_rows
    coupling = coupling / all_rows
    factor = jnp.linalg.cholesky(correlation)

    def solve_lower(matrix):
        return lax.linalg.triangular_solve(factor, matrix, left_side=True, lower=True)

    half_done = solve_lower(coupling)
    projected = solve_lower(half_done.T).T
    return (projected, solve_lower(basis_all), solve_lower(images_all))


def solution(mesh):
    in_specs = (
        P(("row", "col"), None, None),
        P(("row", "col")),
        P(("row", "col")),
        P(None, ("col", "row")),
        P(None, ("col", "row")),
        P(None, ("col", "row")),
    )
    out_specs = (P(), P(None, ("col", "row")), P(None, ("col", "row")))
    return jax.shard_map(local, mesh=mesh, in_specs=in_specs, out_specs=out_specs, check_vma=False)
```

profile of v0, /device:TPU:1, one launch (start us, length us, event | category | flops | bytes accessed | tf_op | source)
XLA Modules:
  0.0 1796.1 jit_solution(15084369518175985899)
XLA Ops:
  7.2 0.0 copy-start
  7.2 0.0 all-gather.2.cloned.1.call-start
  7.2 0.7 all-gather.2.cloned.1.call-update
  7.9 0.0 all-reduce.3.cloned.1.call-start
  8.0 0.7 compare_and_fusion
  8.7 1393.4 %all-gather.2.cloned.1.call-done = bf16[4,524288]{1,0:T(4,128)(2,1)} async-done(((bf16[4,1024]{1,0:T(4,128)(2,1)}), bf16[4,524288]{1,0:T(4,128)(2,1)}) %all-gather.2.cloned.1.call-update) | async-done | bytes 4194320 | tf_op jit(solution)/shard_map/all_gather | solution.py:32
  1402.1 3.6 copy.35
  1405.7 0.0 copy-start.1
  1405.7 0.0 copy-start.4
  1405.7 0.0 copy-start.2
  1405.7 0.0 copy-start.3
  1405.7 1.9 copy-done.1
  1407.6 1.5 dynamic-slice_reduce_fusion
  1409.2 0.1 reshape_reshape.6
  1409.3 0.2 copy.22
  1409.5 0.6 gather_fusion
  1410.1 0.0 copy-done
  1410.1 0.5 fusion.13
  1410.6 1.1 fusion.7
  1411.7 0.0 all-reduce.3.cloned.1.call-update
  1411.8 0.0 reduce-scatter.2.cloned.1.call-start
  1411.8 0.9 dynamic-slice_bitcast_fusion
  1412.7 0.1 reshape_reshape.7
  1412.8 0.1 copy.25
  1412.9 0.6 gather_fusion.1
  1413.5 0.4 fusion.11
  1413.9 1.3 fusion.4
  1415.2 0.0 reduce-scatter.2.cloned.1.call-update
  1415.2 0.0 copy-done.4
  1415.2 0.0 copy-done.2
  1415.2 0.3 fusion.3
  1415.5 128.8 %all-reduce.3.cloned.1.call-done = f32[128,4,128]{2,0,1:T(8,128)} async-done(((f32[128,4,128]{2,0,1:T(8,128)}), f32[128,4,128]{2,0,1:T(8,128)}) %all-reduce.3.cloned.1.call-update) | async-done | bytes 262160 | tf_op jit(solution)/shard_map/psum | solution.py:57
  1544.3 129.5 %reduce-scatter.2.cloned.1.call-done = f32[8,4,128]{2,0,1:T(8,128)} async-done(((f32[256,4,128]{2,0,1:T(8,128)}), f32[8,4,128]{2,0,1:T(8,128)}) %reduce-scatter.2.cloned.1.call-update) | async-done | bytes 16400 | tf_op jit(solution)/shard_map/reduce_scatter | solution.py:56
  1673.8 0.7 add_bitcast_fusion
  1674.5 0.0 copy-done.3
  1674.6 0.3 fusion.1
  1674.9 102.0 %all-reduce = (f32[48,48]{0,1:T(8,128)S(1)}, f32[48,48]{0,1:T(8,128)S(1)}) all-reduce(f32[48,48]{0,1:T(8,128)S(1)} %fusion.3, f32[48,48]{0,1:T(8,128)S(1)} %fusion.1), channel_id=1, replica_groups=mesh['row'=32,'col'=16] {'row','col'}, use_global_device_ids=true, to_apply=%region_0.1 | all-reduce | flops 4608 | bytes 36864 | tf_op jit(solution)/shard_map/psum | solution.py:63
  1776.9 0.1 copy.20
  1777.0 4.4 cholesky.18
  1781.4 0.6 compare_reduce_fusion
  1782.0 0.7 fusion.10
  1782.7 3.7 custom-call.12
  1786.4 1.1 fusion
  1787.4 1.0 fusion.2
  1788.5 0.2 convolution_bitcast_fusion.1
  1788.7 0.2 convolution_bitcast_fusion
  1788.9 0.7 copy.28
  (9 shorter events, 0.1 us)
Async XLA Ops:
  7.2 1402.9 %copy-start = (bf16[24,128,128]{2,1,0:T(8,128)(2,1)S(1)}, bf16[24,128,128]{2,1,0:T(8,128)(2,1)}, u32[]{:S(2)}) copy-start(bf16[24,128,128]{2,1,0:T(8,128)(2,1)} %param.10) | copy-start | bytes 2359300
  7.2 1394.9 %all-gather.2.cloned.1.call-start = ((), (), s32[]{:S(2)}) async-start(), calls=%async_computation.1 | async-start | bytes 4202496 | tf_op jit(solution)/shard_map/all_gather | solution.py:32
  7.9 1536.4 %all-reduce.3.cloned.1.call-start = ((), (), s32[]{:S(2)}) async-start(), calls=%async_computation.2 | async-start | bytes 524288 | tf_op jit(solution)/shard_map/psum | solution.py:57
  1405.7 1.9 copy-start.1
  1405.7 9.5 copy-start.4
  1405.7 9.5 copy-start.2
  1405.7 268.8 %copy-start.3 = (f32[44,1024]{1,0:T(8,128)S(1)}, f32[44,1024]{1,0:T(8,128)}, u32[]{:S(2)}) copy-start(f32[44,1024]{1,0:T(8,128)} %param.15) | copy-start | bytes 540676
  1411.8 262.0 %reduce-scatter.2.cloned.1.call-start = ((), (), s32[]{:S(2)}) async-start(), calls=%async_computation.3 | async-start | bytes 540672 | tf_op jit(solution)/shard_map/reduce_scatter | solution.py:56
Sparse Core Ops, SparseCore 0:
  10.2 1391.8 all-gather.1
  1411.9 132.4 all-reduce.2
  1549.6 124.1 reduce-scatter.1
where the time goes:
time: 1800 us
  waiting for transfers between devices  1650 us (92%)
  blocking collectives  102 us (6%)
    all_gather x1, waiting for transfers between devices, local(): gathered = lax.all_gather(trial_vectors, ('row', 'col'), axis=1, tiled=True)  1390 us
    reduce_scatter x1, waiting for transfers between devices, local(): lax.psum_scatter(col_partial, 'row', scatter_dimension=0, tiled=True)  129 us
    psum x1, waiting for transfers between devices, local(): row_total = lax.psum(row_partial, 'col')  129 us
    psum x1, blocking collectives, local(): lax.psum((rows_product(basis_all, basis_all), rows_product(basis_all, ima...  102 us
  transfers between devices with their start and end apart: 3, of which 3 were waited for; matrix products, arithmetic and copies ran while one was open for 0% of the time, Pallas kernels for 0%

commit v1 on v0

--- a/solution.py
+++ b/solution.py
@@ -61,7 +61,8 @@
     basis_all = jnp.concatenate([basis_old, trial_wide], axis=0)
     images_all = jnp.concatenate([image_old, new_image], axis=0)
     correlation, coupling = lax.psum(
-        (rows_product(basis_all, basis_all), rows_product(basis_all, images_all)), ("row", "col")
+        lax.psum((rows_product(basis_all, basis_all), rows_product(basis_all, images_all)), "col"),
+        "row",
     )
     correlation = correlation / all_rows
     coupling = coupling / all_rows

time: 1800 us -> 1890 us (1.050)
  blocking collectives: 102 us -> 192 us
    psum x0 -> x1, blocking collectives: none -> 143 us  [local(): lax.psum(lax.psum((rows_product(basis_all, basis_all), rows_product(basis...]
    psum x1, blocking collectives: 102 us -> 49.9 us  [local(): lax.psum((rows_product(basis_all, basis_all), rows_product(basis_all, ima...]
where the time goes in v1:
time: 1890 us
  waiting for transfers between devices  1650 us (87%)
  blocking collectives  192 us (10%)
    all_gather x1, waiting for transfers between devices, local(): gathered = lax.all_gather(trial_vectors, ('row', 'col'), axis=1, tiled=True)  1390 us
    psum x1, blocking collectives, local(): lax.psum(lax.psum((rows_product(basis_all, basis_all), rows_product(basis...  143 us
    reduce_scatter x1, waiting for transfers between devices, local(): lax.psum_scatter(col_partial, 'row', scatter_dimension=0, tiled=True)  129 us
    psum x1, waiting for transfers between devices, local(): row_total = lax.psum(row_partial, 'col')  129 us
    psum x1, blocking collectives, local(): lax.psum((rows_product(basis_all, basis_all), rows_product(basis_all, ima...  49.9 us
  transfers between devices with their start and end apart: 3, of which 3 were waited for; matrix products, arithmetic and copies ran while one was open for 0% of the time, Pallas kernels for 0%

profile of v1, /device:TPU:1, one launch (start us, length us, event | category | flops | bytes accessed | tf_op | source)
XLA Modules:
  0.0 1886.5 jit_solution(1180255738579411814)
XLA Ops:
  7.2 0.0 copy-start
  7.2 0.0 all-gather.2.cloned.1.call-start
  7.2 0.7 all-gather.2.cloned.1.call-update
  7.9 0.0 all-reduce.4.cloned.1.call-start
  8.0 0.7 compare_and_fusion
  8.7 1393.4 %all-gather.2.cloned.1.call-done = bf16[4,524288]{1,0:T(4,128)(2,1)} async-done(((bf16[4,1024]{1,0:T(4,128)(2,1)}), bf16[4,524288]{1,0:T(4,128)(2,1)}) %all-gather.2.cloned.1.call-update) | async-done | bytes 4194320 | tf_op jit(solution)/shard_map/all_gather | solution.py:32
  1402.1 3.6 copy.35
  1405.7 0.0 copy-start.1
  1405.7 0.0 copy-start.4
  1405.7 0.0 copy-start.2
  1405.7 0.0 copy-start.3
  1405.7 1.9 copy-done.1
  1407.6 1.5 dynamic-slice_reduce_fusion
  1409.2 0.1 reshape_reshape.6
  1409.3 0.2 copy.22
  1409.5 0.6 gather_fusion
  1410.1 0.0 copy-done
  1410.1 0.5 fusion.13
  1410.6 1.1 fusion.7
  1411.7 0.0 all-reduce.4.cloned.1.call-update
  1411.8 0.0 reduce-scatter.2.cloned.1.call-start
  1411.8 0.9 dynamic-slice_bitcast_fusion
  1412.7 0.1 reshape_reshape.7
  1412.8 0.1 copy.25
  1412.9 0.6 gather_fusion.1
  1413.5 0.4 fusion.11
  1413.9 1.3 fusion.4
  1415.2 0.0 reduce-scatter.2.cloned.1.call-update
  1415.2 0.0 copy-done.4
  1415.2 0.0 copy-done.2
  1415.2 0.3 fusion.3
  1415.5 128.8 %all-reduce.4.cloned.1.call-done = f32[128,4,128]{2,0,1:T(8,128)} async-done(((f32[128,4,128]{2,0,1:T(8,128)}), f32[128,4,128]{2,0,1:T(8,128)}) %all-reduce.4.cloned.1.call-update) | async-done | bytes 262160 | tf_op jit(solution)/shard_map/psum | solution.py:57
  1544.3 129.5 %reduce-scatter.2.cloned.1.call-done = f32[8,4,128]{2,0,1:T(8,128)} async-done(((f32[256,4,128]{2,0,1:T(8,128)}), f32[8,4,128]{2,0,1:T(8,128)}) %reduce-scatter.2.cloned.1.call-update) | async-done | bytes 16400 | tf_op jit(solution)/shard_map/reduce_scatter | solution.py:56
  1673.8 0.7 add_bitcast_fusion
  1674.5 0.0 copy-done.3
  1674.6 0.3 fusion.1
  1674.9 49.9 %all-reduce.1 = (f32[48,48]{0,1:T(8,128)S(1)}, f32[48,48]{0,1:T(8,128)S(1)}) all-reduce(f32[48,48]{0,1:T(8,128)S(1)} %fusion.3, f32[48,48]{0,1:T(8,128)S(1)} %fusion.1), channel_id=1, replica_groups=mesh['row'=32,'col'=16] {'col'}, use_global_device_ids=true, to_apply=%region_0.1 | all-reduce | flops 4608 | bytes 36864 | tf_op jit(solution)/shard_map/psum | solution.py:64
  1724.8 142.5 %all-reduce = (f32[48,48]{0,1:T(8,128)S(1)}, f32[48,48]{0,1:T(8,128)S(1)}) all-reduce(f32[48,48]{0,1:T(8,128)S(1)} %get-tuple-element.16, f32[48,48]{0,1:T(8,128)S(1)} %get-tuple-element.17), channel_id=1, replica_groups=mesh['row'=32,'col'=16] {'row'}, use_global_device_ids=true, to_apply=%region_1.2 | all-reduce | flops 4608 | bytes 36864 | tf_op jit(solution)/shard_map/psum | solution.py:63
  1867.3 0.1 copy.20
  1867.4 4.4 cholesky.18
  1871.8 0.6 compare_reduce_fusion
  1872.5 0.7 fusion.10
  1873.1 3.7 custom-call.12
  1876.8 1.1 fusion
  1877.8 1.0 fusion.2
  1878.9 0.2 convolution_bitcast_fusion.1
  1879.1 0.2 convolution_bitcast_fusion
  1879.3 0.7 copy.28
  (9 shorter events, 0.1 us)
Async XLA Ops:
  7.2 1402.9 %copy-start = (bf16[24,128,128]{2,1,0:T(8,128)(2,1)S(1)}, bf16[24,128,128]{2,1,0:T(8,128)(2,1)}, u32[]{:S(2)}) copy-start(bf16[24,128,128]{2,1,0:T(8,128)(2,1)} %param.10) | copy-start | bytes 2359300
  7.2 1394.9 %all-gather.2.cloned.1.call-start = ((), (), s32[]{:S(2)}) async-start(), calls=%async_computation.1 | async-start | bytes 4202496 | tf_op jit(solution)/shard_map/all_gather | solution.py:32
  7.9 1536.4 %all-reduce.4.cloned.1.call-start = ((), (), s32[]{:S(2)}) async-start(), calls=%async_computation.2 | async-start | bytes 524288 | tf_op jit(solution)/shard_map/psum | solution.py:57
  1405.7 1.9 copy-start.1
  1405.7 9.5 copy-start.4
  1405.7 9.5 copy-start.2
  1405.7 268.8 %copy-start.3 = (f32[44,1024]{1,0:T(8,128)S(1)}, f32[44,1024]{1,0:T(8,128)}, u32[]{:S(2)}) copy-start(f32[44,1024]{1,0:T(8,128)} %param.15) | copy-start | bytes 540676
  1411.8 262.0 %reduce-scatter.2.cloned.1.call-start = ((), (), s32[]{:S(2)}) async-start(), calls=%async_computation.3 | async-start | bytes 540672 | tf_op jit(solution)/shard_map/reduce_scatter | solution.py:56
Sparse Core Ops, SparseCore 0:
  10.2 1391.8 all-gather.1
  1411.9 132.4 all-reduce.3
  1549.6 124.1 reduce-scatter.1

commit v2 on v0

--- a/solution.py
+++ b/solution.py
@@ -54,7 +54,7 @@
     row_partial = place_blocks(local_rows, row_blocks, forward)
     col_partial = place_blocks(local_cols, col_blocks, backward)
     col_share = lax.psum_scatter(col_partial, "row", scatter_dimension=0, tiled=True)
-    row_total = lax.psum(row_partial, "col")
+    row_total = jnp.sum(lax.all_gather(row_partial, "col"), axis=0)
     own_rows = lax.dynamic_slice_in_dim(row_total, col_index * blocks_dev, blocks_dev, 0)
     new_image = (own_rows + col_share).transpose(1, 0, 2).reshape(vec_count, piece_width)
     trial_wide = trial_vectors.astype(jnp.float32)

time: 1800 us -> 1740 us (0.967)
  waiting for transfers between devices: 1650 us -> 1590 us
    psum x1 -> x0, waiting for transfers between devices: 129 us -> none  [local(): row_total = lax.psum(row_partial, 'col')]
    all_gather x0 -> x1, waiting for transfers between devices: none -> 69.2 us  [local(): row_total = jnp.sum(lax.all_gather(row_partial, 'col'), axis=0)]
where the time goes in v2:
time: 1740 us
  waiting for transfers between devices  1590 us (91%)
  blocking collectives  102 us (6%)
    all_gather x1, waiting for transfers between devices, local(): gathered = lax.all_gather(trial_vectors, ('row', 'col'), axis=1, tiled=True)  1390 us
    reduce_scatter x1, waiting for transfers between devices, local(): lax.psum_scatter(col_partial, 'row', scatter_dimension=0, tiled=True)  126 us
    psum x1, blocking collectives, local(): lax.psum((rows_product(basis_all, basis_all), rows_product(basis_all, ima...  102 us
    all_gather x1, waiting for transfers between devices, local(): row_total = jnp.sum(lax.all_gather(row_partial, 'col'), axis=0)  69.2 us
  transfers between devices with their start and end apart: 3, of which 3 were waited for; matrix products, arithmetic and copies ran while one was open for 0% of the time, Pallas kernels for 0%

profile of v2, /device:TPU:1, one launch (start us, length us, event | category | flops | bytes accessed | tf_op | source)
XLA Modules:
  0.0 1735.1 jit_solution(8665098735271536829)
XLA Ops:
  7.2 0.0 copy-start
  7.2 0.0 all-gather.4.cloned.1.call-start
  7.2 0.7 all-gather.4.cloned.1.call-update
  7.9 0.0 all-gather.6.cloned.1.call-start
  8.0 0.7 compare_and_fusion
  8.7 1393.4 %all-gather.4.cloned.1.call-done = bf16[4,524288]{1,0:T(4,128)(2,1)} async-done(((bf16[4,1024]{1,0:T(4,128)(2,1)}), bf16[4,524288]{1,0:T(4,128)(2,1)}) %all-gather.4.cloned.1.call-update) | async-done | bytes 4194320 | tf_op jit(solution)/shard_map/all_gather | solution.py:32
  1402.1 3.6 copy.35
  1405.7 0.0 copy-start.1
  1405.7 0.0 copy-start.4
  1405.7 0.0 copy-start.2
  1405.7 1.9 copy-done.1
  1407.7 1.5 dynamic-slice_reduce_fusion
  1409.2 0.1 reshape_reshape.6
  1409.3 0.2 copy.22
  1409.5 0.6 gather_fusion
  1410.1 0.0 copy-done
  1410.2 0.5 fusion.13
  1410.7 0.0 copy-start.3
  1410.7 1.1 fusion.7
  1411.8 0.0 all-gather.6.cloned.1.call-update
  1411.8 0.0 reduce-scatter.2.cloned.1.call-start
  1411.9 0.9 dynamic-slice_bitcast_fusion
  1412.8 0.1 reshape_reshape.7
  1412.9 0.1 copy.25
  1413.0 0.6 gather_fusion.1
  1413.6 0.4 fusion.11
  1414.0 1.3 fusion.4
  1415.3 0.0 reduce-scatter.2.cloned.1.call-update
  1415.3 0.0 copy-done.4
  1415.3 0.0 copy-done.2
  1415.3 0.3 fusion.3
  1415.6 69.2 %all-gather.6.cloned.1.call-done = f32[2048,4,128]{2,0,1:T(8,128)} async-done(((f32[128,4,128]{2,0,1:T(8,128)}), f32[2048,4,128]{2,0,1:T(8,128)}) %all-gather.6.cloned.1.call-update) | async-done | bytes 4194320 | tf_op jit(solution)/shard_map/all_gather | solution.py:57
  1484.8 2.4 reduce_sum.9
  1487.2 125.6 %reduce-scatter.2.cloned.1.call-done = f32[8,4,128]{2,0,1:T(8,128)} async-done(((f32[256,4,128]{2,0,1:T(8,128)}), f32[8,4,128]{2,0,1:T(8,128)}) %reduce-scatter.2.cloned.1.call-update) | async-done | bytes 16400 | tf_op jit(solution)/shard_map/reduce_scatter | solution.py:56
  1612.8 0.7 add_bitcast_fusion
  1613.6 0.0 copy-done.3
  1613.6 0.3 fusion.1
  1613.9 102.0 %all-reduce = (f32[48,48]{0,1:T(8,128)S(1)}, f32[48,48]{0,1:T(8,128)S(1)}) all-reduce(f32[48,48]{0,1:T(8,128)S(1)} %fusion.3, f32[48,48]{0,1:T(8,128)S(1)} %fusion.1), channel_id=1, replica_groups=mesh['row'=32,'col'=16] {'row','col'}, use_global_device_ids=true, to_apply=%region_0.1 | all-reduce | flops 4608 | bytes 36864 | tf_op jit(solution)/shard_map/psum | solution.py:63
  1715.9 0.1 copy.20
  1716.0 4.4 cholesky.18
  1720.4 0.6 compare_reduce_fusion
  1721.0 0.7 fusion.10
  1721.7 3.7 custom-call.12
  1725.4 1.1 fusion.2
  1726.4 1.0 fusion
  1727.5 0.2 convolution_bitcast_fusion.1
  1727.7 0.2 convolution_bitcast_fusion
  1727.9 0.7 copy.28
  (9 shorter events, 0.1 us)
Async XLA Ops:
  7.2 1403.0 %copy-start = (bf16[24,128,128]{2,1,0:T(8,128)(2,1)S(1)}, bf16[24,128,128]{2,1,0:T(8,128)(2,1)}, u32[]{:S(2)}) copy-start(bf16[24,128,128]{2,1,0:T(8,128)(2,1)} %param.10) | copy-start | bytes 2359300
  7.2 1394.9 %all-gather.4.cloned.1.call-start = ((), (), s32[]{:S(2)}) async-start(), calls=%async_computation.1 | async-start | bytes 4202496 | tf_op jit(solution)/shard_map/all_gather | solution.py:32
  7.9 1476.9 %all-gather.6.cloned.1.call-start = ((), (), s32[]{:S(2)}) async-start(), calls=%async_computation.3 | async-start | bytes 4456448 | tf_op jit(solution)/shard_map/all_gather | solution.py:57
  1405.7 2.0 copy-start.1
  1405.7 9.6 copy-start.4
  1405.7 9.6 copy-start.2
  1410.7 202.9 %copy-start.3 = (f32[44,1024]{1,0:T(8,128)S(1)}, f32[44,1024]{1,0:T(8,128)}, u32[]{:S(2)}) copy-start(f32[44,1024]{1,0:T(8,128)} %param.15) | copy-start | bytes 540676
  1411.8 201.0 %reduce-scatter.2.cloned.1.call-start = ((), (), s32[]{:S(2)}) async-start(), calls=%async_computation.2 | async-start | bytes 540672 | tf_op jit(solution)/shard_map/reduce_scatter | solution.py:56
Sparse Core Ops, SparseCore 0:
  10.2 1391.8 all-gather.3
  1411.9 72.8 all-gather.5
  1489.4 123.3 reduce-scatter.1
